TPU v7x, 32 devices: a whole 2x2x4 slice. The times are simulated.
32 devices in a mesh: lat: 4 (over y, core), lon: 8 (over z, x).
Axes of the slice: x: 2, y: 2, z: 4, core: 2. Of those that a mesh axis runs over, the one named last changes fastest.
Arguments:
- state: float32 [4, 8, 448, 4096], P(None, None, 'lat', 'lon'), may hold values from -6 to 6
- level_courant: float32 [8], replicated, may hold values from 0.05 to 0.3
- damp_table: float32 [16, 2048], replicated, may hold values from 0.05 to 1
- row_flag: int32 [448], P('lat'), may hold values from 0 to 1, as said below
- row_table: int32 [448], P('lat'), may hold values from 0 to 15
- partner: int32 [4096], P('lon'), may hold values from 0 to 4095, each once
Outputs:
- new_state: float32 [4, 8, 448, 4096], P(None, None, 'lat', 'lon')
Inputs may be any that keep to these rules, and one draw needn't show every extreme that they name: `row_flag`: 0 on every row from 112 to 335; each row of the outer quarters is 1 or 0 on its own; the first and the last row are 1. `partner`: a permutation of the columns.
All inputs are finite; a program needn't handle non-finite values.
Results may differ from a plain program's by a relative error of at most 0.00005.
Values sent between devices are 32-bit elements; how exact they have to be, the bound alone decides.
A program may use at most 128 MiB of HBM per device.

v0:
```python
import math
import jax
import jax.numpy as jnp
from jax import lax
from jax.sharding import PartitionSpec as P

coriolis = 0.3
cos_floor = 0.25


def extended(cells, sides, width, closed):
    for axis, dim in sides:
        count = lax.axis_size(axis)
        ends = count if closed else count - 1
        head = lax.slice_in_dim(cells, 0, width, axis=dim)
        tail = lax.slice_in_dim(cells, cells.shape[dim] - width, cells.shape[dim], axis=dim)
        cells = jnp.concatenate(
            [
                lax.ppermute(tail, axis, [(i, (i + 1) % count) for i in range(ends)]),
                cells,
                lax.ppermute(head, axis, [((i + 1) % count, i) for i in range(ends)]),
            ],
            axis=dim,
        )
    return cells


def zonal_pair(stack):
    padded = extended(stack, (("lon", 3),), 1, True)
    return (padded[..., 2:], padded[..., :-2])


def meridional(stack, sign, partner):
    padded = extended(stack, (("lat", 2),), 1, False)
    edge_rows = jnp.concatenate([stack[:, :, :1, :], stack[:, :, -1:, :]], axis=2)
    circle = lax.all_gather(edge_rows, "lon", axis=3, tiled=True)
    across = sign * jnp.take(circle, partner, axis=3)
    southward = padded[:, :, :-2, :]
    northward = padded[:, :, 2:, :]
    at_south = lax.axis_index("lat") == 0
    at_north = lax.axis_index("lat") == lax.axis_size("lat") - 1
    southward = southward.at[:, :, 0, :].set(
        jnp.where(at_south, across[:, :, 0, :], southward[:, :, 0, :])
    )
    northward = northward.at[:, :, -1, :].set(
        jnp.where(at_north, across[:, :, 1, :], northward[:, :, -1, :])
    )
    return (northward, southward)


def angle_table(size_a, size_b, modulus):
    product = (
        jnp.arange(size_a, dtype=jnp.int32)[:, None]
        * jnp.arange(size_b, dtype=jnp.int32)[None, :]
        % modulus
    )
    angle = product.astype(jnp.float32) * (2.0 * math.pi / modulus)
    return (jnp.cos(angle), jnp.sin(angle))


def fourier_damp(rows_in, damping):
    count_b, count_r, length = rows_in.shape
    inner_len = 128
    outer_len = length // inner_len
    highest = lax.Precision.HIGHEST
    small_cos, small_sin = angle_table(outer_len, outer_len, outer_len)
    twid_cos, twid_sin = angle_table(outer_len, inner_len, length)
    large_cos, large_sin = angle_table(inner_len, inner_len, inner_len)
    grid = rows_in.reshape(count_b, count_r, outer_len, inner_len)
    a_real = jnp.einsum("brpq,kp->brkq", grid, small_cos, precision=highest)
    a_imag = -jnp.einsum("brpq,kp->brkq", grid, small_sin, precision=highest)
    b_real = a_real * twid_cos + a_imag * twid_sin
    b_imag = a_imag * twid_cos - a_real * twid_sin
    f_real = jnp.einsum("brkq,qm->brkm", b_real, large_cos, precision=highest) + jnp.einsum(
        "brkq,qm->brkm", b_imag, large_sin, precision=highest
    )
    f_imag = jnp.einsum("brkq,qm->brkm", b_imag, large_cos, precision=highest) - jnp.einsum(
        "brkq,qm->brkm", b_real, large_sin, precision=highest
    )
    weight = jnp.transpose(damping.reshape(count_r, inner_len, outer_len), (0, 2, 1))[None]
    f_real = f_real * weight
    f_imag = f_imag * weight
    z_real = jnp.einsum("brkq,qm->brkm", f_real, large_cos, precision=highest) - jnp.einsum(
        "brkq,qm->brkm", f_imag, large_sin, precision=highest
    )
    z_imag = jnp.einsum("brkq,qm->brkm", f_imag, large_cos, precision=highest) + jnp.einsum(
        "brkq,qm->brkm", f_real, large_sin, precision=highest
    )
    w_real = z_real * twid_cos - z_imag * twid_sin
    w_imag = z_imag * twid_cos + z_real * twid_sin
    result = jnp.einsum("brkq,kp->brpq", w_real, small_cos, precision=highest) - jnp.einsum(
        "brkq,kp->brpq", w_imag, small_sin, precision=highest
    )
    return (result / length).reshape(count_b, count_r, length)


def damp_half(values, row_codes, damp_table):
    active = jnp.any(row_codes > 0)

    def run_filter(inputs):
        table_count = damp_table.shape[0]
        row_count = row_codes.shape[0]
        pick = (row_codes[:, None] - 1 == jnp.arange(table_count, dtype=jnp.int32)[None, :]).astype(
            jnp.float32
        )
        half_damp = jnp.dot(
            pick, damp_table, precision=lax.Precision.HIGHEST, preferred_element_type=jnp.float32
        )
        full_damp = jnp.concatenate(
            [jnp.ones((row_count, 1), jnp.float32), half_damp, jnp.flip(half_damp[:, :-1], axis=1)],
            axis=1,
        )
        shaped = fourier_damp(inputs, full_damp)
        return jnp.where((row_codes > 0)[None, :, None], shaped, inputs)

    return lax.cond(active, run_filter, lambda kept: kept, values)


def regroup(row_block, row_codes, damp_table):
    fields_n, levels_n, rows_n, cols_n = row_block.shape
    half_rows = rows_n // 2
    merged = row_block.reshape(fields_n * levels_n, rows_n, cols_n)
    circles = lax.all_to_all(merged, "lon", split_axis=0, concat_axis=2, tiled=True)
    first_part = damp_half(circles[:, :half_rows, :], row_codes[:half_rows], damp_table)
    second_part = damp_half(circles[:, half_rows:, :], row_codes[half_rows:], damp_table)
    joined = jnp.concatenate([first_part, second_part], axis=1)
    returned = lax.all_to_all(joined, "lon", split_axis=2, concat_axis=0, tiled=True)
    return returned.reshape(fields_n, levels_n, rows_n, cols_n)


def per_device(state, level_courant, damp_table, row_flag, row_table, partner):
    fields_n, levels_n, rows_n, cols_n = state.shape
    whole_rows = rows_n * lax.axis_size("lat")
    row_pos = (lax.axis_index("lat") * rows_n + jnp.arange(rows_n, dtype=jnp.int32)).astype(
        jnp.float32
    )
    latitude = -jnp.pi / 2 + jnp.pi * (row_pos + 0.5) / whole_rows
    cos_lat = jnp.cos(latitude)[:, None]
    sin_lat = jnp.sin(latitude)[:, None]
    metric = 1.0 / jnp.maximum(cos_lat, cos_floor)
    courant = level_courant[:, None, None]
    pressure, wind_u, wind_v, thermo = (state[0], state[1], state[2], state[3])
    scalars = jnp.stack([pressure, thermo])
    eastward, westward = zonal_pair(scalars)
    northward, southward = meridional(scalars, 1.0, partner)
    tend_u = -courant * metric * (eastward[0] - westward[0]) * 0.5 + coriolis * sin_lat * wind_v
    tend_v = -courant * (northward[0] - southward[0]) * 0.5 - coriolis * sin_lat * wind_u
    u_new = wind_u + tend_u
    v_new = wind_v + tend_v
    flux = v_new * cos_lat
    u_east, u_west = zonal_pair(u_new[None])
    f_north, f_south = meridional(flux[None], -1.0, partner)
    divergence = (
        courant * metric * ((u_east[0] - u_west[0]) * 0.5 + (f_north[0] - f_south[0]) * 0.5)
    )
    tend_t = (
        -courant * metric * u_new * (eastward[1] - westward[1]) * 0.5
        - courant * v_new * (northward[1] - southward[1]) * 0.5
    )
    increments = jnp.stack([-divergence, tend_u, tend_v, tend_t])
    row_codes = jnp.where(row_flag == 1, row_table + 1, 0)
    increments = regroup(increments, row_codes, damp_table)
    return state + increments


def solution(mesh):
    placed = (P(None, None, "lat", "lon"), P(), P(), P("lat"), P("lat"), P("lon"))
    return jax.shard_map(
        per_device,
        mesh=mesh,
        in_specs=placed,
        out_specs=P(None, None, "lat", "lon"),
        check_vma=False,
    )
```

profile of v0, /device:TPU:0, one launch (start us, length us, event | category | flops | bytes accessed | tf_op | source)
XLA Modules:
  0.0 609.3 jit_solution(8997078380388542498)
XLA Ops:
  9.7 6.0 collective-permute-start
  16.1 31.4 %all_gather.6 = f32[2,8,2,4096]{3,1,2,0:T(8,128)S(1)} all-gather(f32[2,8,2,512]{3,1,2,0:T(8,128)S(1)} %pad_maximum_fusion.14), channel_id=1, replica_groups=mesh['lat'=4,'lon'=8] {'lon'}, dimensions={3}, use_global_device_ids=true | all-gather | bytes 589824 | tf_op jit(solution)/shard_map/all_gather | solution.py:36
  47.5 7.9 %copy.330 = f32[2,8,2,4096]{1,2,3,0:T(2,128)} copy(f32[2,8,2,4096]{3,1,2,0:T(8,128)S(1)} %all_gather.6) | data formatting | bytes 1048576 | tf_op jit(solution)/shard_map/all_gather | solution.py:36
  55.5 5.5 gather_fusion
  63.7 6.4 %pad_maximum_fusion.4 = (f32[2,8,112,512]{3,2,1,0:T(8,128)}, f32[2,8,112,512]{3,2,1,0:T(8,128)}) fusion(f32[2,8,1,512]{3,2,1,0:T(1,128)S(1)} %collective-permute-done.4, f32[1,8,112,512]{3,2,1,0:T(8,128)} %copy-done.8, f32[1,8,112,512]{3,2,1,0:T(8,128)S(1)} %get-tuple-element.94, f32[2,8,1,512]{3,2,1,0:T(1,128)S(1)} %collective-permute-done.5), kind=kLoop, calls=%fused_computation.277 | loop fusion | flops 3670016 | bytes 11075584 | tf_op jit(solution)/shard_map/concatenate | solution.py:17
  73.6 5.4 broadcast_multiply_fusion
  84.7 30.7 %all_gather.7 = f32[1,8,2,4096]{3,1,2,0:T(8,128)S(1)} all-gather(f32[1,8,2,512]{3,1,2,0:T(8,128)S(1)} %pad_maximum_fusion.16), channel_id=1, replica_groups=mesh['lat'=4,'lon'=8] {'lon'}, dimensions={3}, use_global_device_ids=true | all-gather | bytes 294912 | tf_op jit(solution)/shard_map/all_gather | solution.py:36
  115.4 4.3 copy.334
  119.7 3.7 gather_fusion.1
  123.5 8.2 %fusion.262 = (f32[1,8,112,512]{3,2,1,0:T(8,128)}, f32[1,8,112,512]{3,2,1,0:T(8,128)S(1)}, f32[1,8,112,512]{3,2,1,0:T(8,128)}) fusion(f32[2,8,112,512]{3,2,1,0:T(8,128)} %scatter.15, f32[2,8,112,512]{3,2,1,0:T(8,128)} %scatter.14, f32[2,8,112,1]{3,2,1,0:T(8,128)} %copy.327, f32[1,8,112,512]{3,2,1,0:T(8,128)} %copy-done.8, ...), kind=kLoop, calls=%fused_computation.282 | loop fusion | flops 11010048 | bytes 18368480 | tf_op jit(solution)/shard_map/sub | solution.py:157
  132.0 4.6 collective-permute-start.2
  140.7 9.7 %collective-permute-done.2 = f32[1,8,112,1]{3,2,1,0:T(8,128)S(1)} collective-permute-done((f32[1,8,112,1]{3,2,1,0:T(8,128)S(1)}, f32[1,8,112,1]{3,2,1,0:T(8,128)S(1)}, u32[]{:S(2)}, u32[]{:S(2)}) %collective-permute-start.2) | collective-permute-done | bytes 3616 | tf_op jit(solution)/shard_map/ppermute | solution.py:21
  150.4 4.2 fusion.276
  154.7 3.5 pad_maximum_fusion.1
  158.2 5.1 all-to-all-start
  165.4 156.9 %all-to-all-done = f32[32,112,512]{2,1,0:T(8,128)} async-done(((f32[32,112,512]{2,1,0:T(8,128)}), f32[32,112,512]{2,1,0:T(8,128)}, u32[]{:S(2)}, u32[]{:S(2)}) %all-to-all-start) | async-done | bytes 7340064 | tf_op jit(solution)/shard_map/all_to_all | solution.py:123
  322.4 4.3 copy.364
  326.7 3.9 fusion.289
  330.6 76.1 %conditional.2 = (f32[4,56,4096]{1,0,2:T(4,128)}) conditional(s32[]{:T(128)} %convert_element_type.123, f32[4,56,4096]{2,1,0:T(8,128)} %get-tuple-element.92, (s32[56]{0:T(128)S(1)}, f32[4,56,4096]{2,1,0:T(8,128)}, f32[16,2048]{1,0:T(8,128)S(1)}) %tuple.62), branch_computations={%region_1.2_spmd, %region_2.3_spmd} | conditional | flops 12735988736 | bytes 230196096 | solution.py:116
  333.5 3.5 fusion
  337.0 3.5 fusion.2
  340.6 5.3 fusion.4
  350.8 7.7 %subtract_multiply_fusion = f32[4,56,32,128]{3,2,1,0:T(8,128)S(1)} fusion(f32[4,56,32,128]{3,2,1,0:T(8,128)} %fusion.4, f32[56,32,128]{2,1,0:T(8,128)S(1)} %copy.319, f32[32,4,56,128]{3,0,2,1:T(8,128)} %copy-done.2, f32[32,4,56,128]{3,0,2,1:T(8,128)} %copy-done, f32[32,128]{1,0:T(8,128)S(1)} %get-tuple-element.88, f32[32,128]{1,0:T(8,128)S(1)} %get-tuple-element.89), kind=kOutput, calls=%fused_computation.23 | convolution fusion | flops 1415020544 | bytes 15630336 | tf_op jit(solution)/shard_map/cond/branch_1_fun/brkq,qm->brkm/dot_general | solution.py:77
  365.2 3.4 add_multiply_fusion
  368.7 3.5 convolution_add_fusion
  372.1 3.4 fusion.40
  382.3 5.2 multiply_bitcast_fusion
  387.6 4.8 reshape.392
  392.4 5.6 broadcast_select_fusion
  398.0 8.3 %copy.357 = f32[4,56,4096]{1,0,2:T(4,128)} copy(f32[4,56,4096]{2,1,0:T(8,128)} %broadcast_select_fusion) | data formatting | bytes 7340032 | tf_op jit(solution)/shard_map/cond | solution.py:116
  406.7 75.8 %conditional.3 = (f32[4,56,4096]{1,0,2:T(4,128)}) conditional(s32[]{:T(128)} %convert_element_type.125, f32[4,56,4096]{2,1,0:T(8,128)} %get-tuple-element.93, (s32[56]{0:T(128)S(1)}, f32[4,56,4096]{2,1,0:T(8,128)}, f32[16,2048]{1,0:T(8,128)S(1)}) %tuple.63), branch_computations={%region_4.5_spmd, %region_5.6_spmd} | conditional | flops 12735988736 | bytes 230196096 | solution.py:116
  409.5 3.5 fusion.130
  413.0 3.5 fusion.132
  416.5 5.2 fusion.134
  426.4 7.7 %subtract_multiply_fusion.1 = f32[4,56,32,128]{3,2,1,0:T(8,128)S(1)} fusion(f32[4,56,32,128]{3,2,1,0:T(8,128)} %fusion.134, f32[56,32,128]{2,1,0:T(8,128)S(1)} %copy.323, f32[32,4,56,128]{3,0,2,1:T(8,128)} %copy-done.6, f32[32,4,56,128]{3,0,2,1:T(8,128)} %copy-done.4, f32[32,128]{1,0:T(8,128)S(1)} %get-tuple-element.90, f32[32,128]{1,0:T(8,128)S(1)} %get-tuple-element.91), kind=kOutput, calls=%fused_computation.155 | convolution fusion | flops 1415020544 | bytes 15630336 | tf_op jit(solution)/shard_map/cond/branch_1_fun/brkq,qm->brkm/dot_general | solution.py:77
  437.5 3.4 fusion.136
  440.9 3.4 add_multiply_fusion.1
  444.3 3.5 convolution_add_fusion.1
  447.8 3.4 fusion.170
  454.6 3.8 fusion.142
  458.4 5.3 multiply_bitcast_fusion.1
  463.7 4.8 reshape.395
  468.5 5.6 broadcast_select_fusion.1
  474.1 8.2 %copy.359 = f32[4,56,4096]{1,0,2:T(4,128)} copy(f32[4,56,4096]{2,1,0:T(8,128)} %broadcast_select_fusion.1) | data formatting | bytes 7340032 | tf_op jit(solution)/shard_map/cond | solution.py:116
  482.5 8.2 %pad_maximum_fusion = f32[4,112,4096]{1,0,2:T(4,128)S(1)} fusion(f32[4,56,4096]{1,0,2:T(4,128)} %get-tuple-element.80, f32[4,56,4096]{1,0,2:T(4,128)} %get-tuple-element.79), kind=kLoop, calls=%fused_computation.266 | loop fusion | flops 1835008 | bytes 14680064 | tf_op jit(solution)/shard_map/concatenate | solution.py:126
  490.8 98.2 %all_to_all.33 = f32[4,112,4096]{1,0,2:T(4,128)} all-to-all(f32[4,112,4096]{1,0,2:T(4,128)S(1)} %pad_maximum_fusion), channel_id=1, replica_groups=mesh['lat'=4,'lon'=8] {'lon'}, dimensions={2} | all-to-all | bytes 14680064 | tf_op jit(solution)/shard_map/all_to_all | solution.py:127
  588.9 9.5 %copy.339 = f32[8,4,112,512]{3,2,1,0:T(8,128)} copy(f32[8,4,112,512]{2,1,3,0:T(4,128)} %bitcast.199) | data formatting | bytes 14680064 | tf_op jit(solution)/shard_map/all_to_all | solution.py:127
  598.5 10.6 %bitcast_add_fusion = f32[4,8,112,512]{3,2,1,0:T(8,128)} fusion(f32[4,8,112,512]{3,2,1,0:T(8,128)} %param.18, f32[4,8,112,512]{3,2,1,0:T(8,128)} %bitcast.206), kind=kLoop, calls=%fused_computation.268 | loop fusion | flops 1835008 | bytes 22020096 | tf_op jit(solution)/shard_map/add | solution.py:163
  (117 shorter events, 62.3 us)
Async XLA Ops:
  2.6 5.7 copy-start.8
  2.6 61.0 %collective-permute-start.4 = (f32[2,8,1,512]{3,2,1,0:T(1,128)S(1)}, f32[2,8,1,512]{3,2,1,0:T(1,128)S(1)}, u32[]{:S(2)}, u32[]{:S(2)}) collective-permute-start(f32[2,8,1,512]{3,2,1,0:T(1,128)S(1)} %get-tuple-element.100), channel_id=1, source_target_pairs={{8,0},{16,8},{24,16},{9,1},{17,9},{25,17},{10,2},{18,10},{26,18},{... | collective-permute-start | bytes 98312 | tf_op jit(solution)/shard_map/ppermute | solution.py:21
  3.9 12.1 %copy-start.16 = (s32[512]{0:T(512)S(1)}, s32[512]{0:T(512)}, u32[]{:S(2)}) copy-start(s32[512]{0:T(512)} %param.23) | copy-start | bytes 6148
  4.0 59.7 %collective-permute-start.5 = (f32[2,8,1,512]{3,2,1,0:T(1,128)S(1)}, f32[2,8,1,512]{3,2,1,0:T(1,128)S(1)}, u32[]{:S(2)}, u32[]{:S(2)}) collective-permute-start(f32[2,8,1,512]{3,2,1,0:T(1,128)S(1)} %get-tuple-element.101), channel_id=1, source_target_pairs={{0,8},{8,16},{16,24},{1,9},{9,17},{17,25},{2,10},{10,18},{18,26},{... | collective-permute-start | bytes 98312 | tf_op jit(solution)/shard_map/ppermute | solution.py:19
  9.7 52.3 %collective-permute-start = (f32[2,8,112,1]{2,1,3,0:T(8,128)S(1)}, f32[2,8,112,1]{2,1,3,0:T(8,128)S(1)}, u32[]{:S(2)}, u32[]{:S(2)}) collective-permute-start(f32[2,8,112,1]{2,1,3,0:T(8,128)S(1)} %copy.360), channel_id=1, source_target_pairs={{1,0},{2,1},{3,2},{4,3},{5,4},{6,5},{7,6},{0,7},{9,8},{10,9},{11,1... | collective-permute-start | bytes 21512 | tf_op jit(solution)/shard_map/ppermute | solution.py:21
  16.0 46.4 %collective-permute-start.1 = (f32[2,8,112,1]{2,1,3,0:T(8,128)S(1)}, f32[2,8,112,1]{2,1,3,0:T(8,128)S(1)}, u32[]{:S(2)}, u32[]{:S(2)}) collective-permute-start(f32[2,8,112,1]{2,1,3,0:T(8,128)S(1)} %copy.361), channel_id=1, source_target_pairs={{0,1},{1,2},{2,3},{3,4},{4,5},{5,6},{6,7},{7,0},{8,9},{9,10},{10,1... | collective-permute-start | bytes 21512 | tf_op jit(solution)/shard_map/ppermute | solution.py:19
  47.5 14.3 %copy-start.17 = (f32[8]{0:T(128)S(1)}, f32[8]{0:T(128)}, u32[]{:S(2)}) copy-start(f32[8]{0:T(128)} %param.19) | copy-start | bytes 100
  79.1 1.2 copy-start.11
  80.3 56.3 %collective-permute-start.6 = (f32[1,8,1,512]{3,2,1,0:T(1,128)S(1)}, f32[1,8,1,512]{3,2,1,0:T(1,128)S(1)}, u32[]{:S(2)}, u32[]{:S(2)}) collective-permute-start(f32[1,8,1,512]{3,2,1,0:T(1,128)S(1)} %get-tuple-element.105), channel_id=1, source_target_pairs={{8,0},{16,8},{24,16},{9,1},{17,9},{25,17},{10,2},{18,10},{26,18},{... | collective-permute-start | bytes 49160 | tf_op jit(solution)/shard_map/ppermute | solution.py:21
  81.6 55.0 %collective-permute-start.7 = (f32[1,8,1,512]{3,2,1,0:T(1,128)S(1)}, f32[1,8,1,512]{3,2,1,0:T(1,128)S(1)}, u32[]{:S(2)}, u32[]{:S(2)}) collective-permute-start(f32[1,8,1,512]{3,2,1,0:T(1,128)S(1)} %get-tuple-element.104), channel_id=1, source_target_pairs={{0,8},{8,16},{16,24},{1,9},{9,17},{17,25},{2,10},{10,18},{18,26},{... | collective-permute-start | bytes 49160 | tf_op jit(solution)/shard_map/ppermute | solution.py:19
  123.5 13.1 %copy-start.12 = (f32[1,8,112,512]{3,2,1,0:T(8,128)S(1)}, f32[1,8,112,512]{3,2,1,0:T(8,128)}, u32[]{:S(2)}) copy-start(f32[1,8,112,512]{3,2,1,0:T(8,128)} %copy-done.11) | copy-start | bytes 5505028
  131.8 6.6 %copy-start.10 = (f32[1,8,112,512]{3,2,1,0:T(8,128)}, f32[1,8,112,512]{3,2,1,0:T(8,128)S(1)}, u32[]{:S(2)}) copy-start(f32[1,8,112,512]{3,2,1,0:T(8,128)S(1)} %get-tuple-element.86) | copy-start | bytes 5505028
  132.0 18.4 %collective-permute-start.2 = (f32[1,8,112,1]{3,2,1,0:T(8,128)S(1)}, f32[1,8,112,1]{3,2,1,0:T(8,128)S(1)}, u32[]{:S(2)}, u32[]{:S(2)}) collective-permute-start(f32[1,8,112,1]{3,2,1,0:T(8,128)S(1)} %get-tuple-element.106), channel_id=1, source_target_pairs={{1,0},{2,1},{3,2},{4,3},{5,4},{6,5},{7,6},{0,7},{9,8},{10,9},{11,1... | collective-permute-start | bytes 10760 | tf_op jit(solution)/shard_map/ppermute | solution.py:21
  136.6 13.8 %collective-permute-start.3 = (f32[1,8,112,1]{3,2,1,0:T(8,128)S(1)}, f32[1,8,112,1]{3,2,1,0:T(8,128)}, u32[]{:S(2)}, u32[]{:S(2)}) collective-permute-start(f32[1,8,112,1]{3,2,1,0:T(8,128)S(1)} %get-tuple-element.107), channel_id=1, source_target_pairs={{0,1},{1,2},{2,3},{3,4},{4,5},{5,6},{6,7},{7,0},{8,9},{9,10},{10,1... | collective-permute-start | bytes 10760 | tf_op jit(solution)/shard_map/ppermute | solution.py:19
  150.4 4.2 copy-start.9
  150.4 4.2 copy-start.13
  150.4 4.4 copy-start.14
  158.2 5.1 copy-start.18
  158.2 5.1 copy-start.19
  158.2 164.2 %all-to-all-start = ((f32[32,112,512]{2,1,0:T(8,128)}), f32[32,112,512]{2,1,0:T(8,128)}, u32[]{:S(2)}, u32[]{:S(2)}) async-start(f32[32,112,512]{2,1,0:T(8,128)} %bitcast.204), calls=%async_computation | async-start | bytes 14680064 | tf_op jit(solution)/shard_map/all_to_all | solution.py:123
  326.7 3.9 copy-start.15
  337.0 3.5 copy-start
  340.5 5.3 copy-start.2
  358.5 3.3 copy-start.1
  358.5 3.3 copy-start.3
  413.0 3.5 copy-start.4
  416.5 5.2 copy-start.6
  434.2 3.3 copy-start.5
  434.2 3.3 copy-start.7
where the time goes:
time: 619 us; the launch traced here: 609 us
  waiting for transfers between devices  167 us (27%)
  blocking collectives  160 us (26%)
  matrix products  99.1 us (16%)
  local copies, waits for them, and re-layouts  93.7 us (15%)
  other arithmetic  62.2 us (10%)
  starting transfers between devices  24.4 us (4%)
    all_to_all x1, waiting for transfers between devices, regroup(): lax.all_to_all(merged, 'lon', split_axis=0, concat_axis=2, tiled=True)  157 us
    all_to_all x1, blocking collectives, regroup(): lax.all_to_all(joined, 'lon', split_axis=2, concat_axis=0, tiled=True)  98.2 us
    all_gather x2, blocking collectives, meridional(): circle = lax.all_gather(edge_rows, 'lon', axis=3, tiled=True)  62.2 us
    cond x2, local copies, waits for them, and re-layouts, damp_half(): return lax.cond(active, run_filter, lambda kept: kept, values)  16.6 us
    dot_general x2, matrix products, fourier_damp(): jnp.einsum('brkq,qm->brkm', b_real, large_sin, precision=highest)  15.4 us
    ppermute x4, starting transfers between devices, extended(): lax.ppermute(head, axis, [((i + 1) % count, i) for i in range(ends)])  13.2 us
  transfers between devices with their start and end apart: 9, of which 2 were waited for; matrix products, arithmetic and copies ran while one was open for 7% of the time, Pallas kernels for 0%

commit v1 on v0

--- a/solution.py
+++ b/solution.py
@@ -6,6 +6,17 @@
 
 coriolis = 0.3
 cos_floor = 0.25
+
+
+def split_up(array, dim, size):
+    before, after = (array.shape[:dim], array.shape[dim + 1 :])
+    return jnp.moveaxis(array.reshape(*before, size, -1, *after), dim, 0)
+
+
+def in_order(blocks, dim):
+    blocks = jnp.moveaxis(blocks, 0, dim)
+    shape = blocks.shape
+    return blocks.reshape(*shape[:dim], shape[dim] * shape[dim + 1], *shape[dim + 2 :])
 
 
 def extended(cells, sides, width, closed):
@@ -120,7 +131,17 @@
     fields_n, levels_n, rows_n, cols_n = row_block.shape
     half_rows = rows_n // 2
     merged = row_block.reshape(fields_n * levels_n, rows_n, cols_n)
-    circles = lax.all_to_all(merged, "lon", split_axis=0, concat_axis=2, tiled=True)
+    count_2, index = (lax.axis_size("lon"), lax.axis_index("lon"))
+    tiles = split_up(merged, 0, count_2)
+    result_2 = tiles
+    for lap in range(1, count_2):
+        target, source = ((index + lap) % count_2, (index - lap) % count_2)
+        sent = lax.dynamic_index_in_dim(tiles, target, 0)
+        partner_block = lax.ppermute(
+            sent, "lon", [(i_2, (i_2 + lap) % count_2) for i_2 in range(count_2)]
+        )
+        result_2 = lax.dynamic_update_slice_in_dim(result_2, partner_block, source, axis=0)
+    circles = in_order(result_2, 2)
     first_part = damp_half(circles[:, :half_rows, :], row_codes[:half_rows], damp_table)
     second_part = damp_half(circles[:, half_rows:, :], row_codes[half_rows:], damp_table)
     joined = jnp.concatenate([first_part, second_part], axis=1)

time: 619 us -> 647 us (1.045)
  blocking collectives: 160 us -> 206 us
  waiting for transfers between devices: 167 us -> 126 us
  local copies, waits for them, and re-layouts: 93.7 us -> 115 us
    all_to_all x1 -> x0, waiting for transfers between devices: 157 us -> none  [regroup(): lax.all_to_all(merged, 'lon', split_axis=0, concat_axis=2, tiled=True)]
    ppermute x0 -> x7, waiting for transfers between devices: none -> 116 us  [regroup(): lax.ppermute(sent, 'lon', [(i_2, (i_2 + lap) % count_2) for i_2 in range(...]
    all_to_all x1, blocking collectives: 98.2 us -> 144 us  [regroup(): lax.all_to_all(joined, 'lon', split_axis=2, concat_axis=0, tiled=True)]
    dynamic_update_slice x0 -> x6, local copies, waits for them, and re-layouts: none -> 13 us  [regroup(): lax.dynamic_update_slice_in_dim(result_2, partner_block, source, axis=0)]
    ppermute x0 -> x7, starting transfers between devices: none -> 9.51 us  [regroup(): lax.ppermute(sent, 'lon', [(i_2, (i_2 + lap) % count_2) for i_2 in range(...]
  transfers between devices with their start and end apart: 9 -> 15, of which waited for: 2 -> 6; matrix products, arithmetic and copies ran while one was open for 7% -> 8% of each run, Pallas kernels for 0% -> 0%
where the time goes in v1:
time: 647 us; the launch traced here: 638 us
  blocking collectives  206 us (32%)
  waiting for transfers between devices  126 us (19%)
  local copies, waits for them, and re-layouts  115 us (18%)
  matrix products  99.1 us (15%)
  other arithmetic  59.7 us (9%)
  starting transfers between devices  28.8 us (4%)
    all_to_all x1, blocking collectives, regroup(): lax.all_to_all(joined, 'lon', split_axis=2, concat_axis=0, tiled=True)  144 us
    ppermute x7, waiting for transfers between devices, regroup(): lax.ppermute(sent, 'lon', [(i_2, (i_2 + lap) % count_2) for i_2 in range(...  116 us
    all_gather x2, blocking collectives, meridional(): circle = lax.all_gather(edge_rows, 'lon', axis=3, tiled=True)  62.2 us
    cond x2, local copies, waits for them, and re-layouts, damp_half(): return lax.cond(active, run_filter, lambda kept: kept, values)  16.6 us
    dot_general x2, matrix products, fourier_damp(): jnp.einsum('brkq,qm->brkm', b_real, large_sin, precision=highest)  15.4 us
    ppermute x4, starting transfers between devices, extended(): lax.ppermute(head, axis, [((i + 1) % count, i) for i in range(ends)])  13.2 us
    dynamic_update_slice x6, local copies, waits for them, and re-layouts, regroup(): lax.dynamic_update_slice_in_dim(result_2, partner_block, source, axis=0)  13 us
  transfers between devices with their start and end apart: 15, of which 6 were waited for; matrix products, arithmetic and copies ran while one was open for 8% of the time, Pallas kernels for 0%

profile of v1, /device:TPU:0, one launch (start us, length us, event | category | flops | bytes accessed | tf_op | source)
XLA Modules:
  0.0 637.7 jit_solution(7423982656110976118)
XLA Ops:
  9.7 6.0 collective-permute-start
  16.1 31.4 %all_gather.6 = f32[2,8,2,4096]{3,1,2,0:T(8,128)S(1)} all-gather(f32[2,8,2,512]{3,1,2,0:T(8,128)S(1)} %pad_maximum_fusion.14), channel_id=1, replica_groups=mesh['lat'=4,'lon'=8] {'lon'}, dimensions={3}, use_global_device_ids=true | all-gather | bytes 589824 | tf_op jit(solution)/shard_map/all_gather | solution.py:47
  47.5 7.9 %copy.379 = f32[2,8,2,4096]{1,2,3,0:T(2,128)} copy(f32[2,8,2,4096]{3,1,2,0:T(8,128)S(1)} %all_gather.6) | data formatting | bytes 1048576 | tf_op jit(solution)/shard_map/all_gather | solution.py:47
  55.5 5.5 gather_fusion
  63.7 6.4 %pad_maximum_fusion.4 = (f32[2,8,112,512]{3,2,1,0:T(8,128)}, f32[2,8,112,512]{3,2,1,0:T(8,128)}) fusion(f32[2,8,1,512]{3,2,1,0:T(1,128)S(1)} %collective-permute-done.4, f32[1,8,112,512]{3,2,1,0:T(8,128)} %copy-done.9, f32[1,8,112,512]{3,2,1,0:T(8,128)S(1)} %get-tuple-element.101, f32[2,8,1,512]{3,2,1,0:T(1,128)S(1)} %collective-permute-done.5), kind=kLoop, calls=%fused_computation.277 | loop fusion | flops 3670016 | bytes 11075584 | tf_op jit(solution)/shard_map/concatenate | solution.py:28
  73.7 5.4 broadcast_multiply_fusion
  84.8 30.7 %all_gather.7 = f32[1,8,2,4096]{3,1,2,0:T(8,128)S(1)} all-gather(f32[1,8,2,512]{3,1,2,0:T(8,128)S(1)} %pad_maximum_fusion.16), channel_id=1, replica_groups=mesh['lat'=4,'lon'=8] {'lon'}, dimensions={3}, use_global_device_ids=true | all-gather | bytes 294912 | tf_op jit(solution)/shard_map/all_gather | solution.py:47
  115.5 4.3 copy.383
  119.8 3.7 gather_fusion.1
  123.6 8.2 %fusion.262 = (f32[1,8,112,512]{3,2,1,0:T(8,128)}, f32[1,8,112,512]{3,2,1,0:T(8,128)S(1)}, f32[1,8,112,512]{3,2,1,0:T(8,128)}) fusion(f32[2,8,112,512]{3,2,1,0:T(8,128)} %scatter.15, f32[2,8,112,512]{3,2,1,0:T(8,128)} %scatter.14, f32[2,8,112,1]{3,2,1,0:T(8,128)} %copy.376, f32[1,8,112,512]{3,2,1,0:T(8,128)} %copy-done.9, ...), kind=kLoop, calls=%fused_computation.282 | loop fusion | flops 11010048 | bytes 18368480 | tf_op jit(solution)/shard_map/sub | solution.py:178
  132.1 4.6 collective-permute-start.2
  140.4 10.0 %collective-permute-done.2 = f32[1,8,112,1]{3,2,1,0:T(8,128)S(1)} collective-permute-done((f32[1,8,112,1]{3,2,1,0:T(8,128)S(1)}, f32[1,8,112,1]{3,2,1,0:T(8,128)S(1)}, u32[]{:S(2)}, u32[]{:S(2)}) %collective-permute-start.2) | collective-permute-done | bytes 3616 | tf_op jit(solution)/shard_map/ppermute | solution.py:32
  150.5 4.2 fusion.276
  160.9 21.4 %collective-permute-done.8 = f32[1,4,112,512]{3,2,1,0:T(8,128)} collective-permute-done((f32[1,4,112,512]{3,2,1,0:T(8,128)S(1)}, f32[1,4,112,512]{3,2,1,0:T(8,128)}, u32[]{:S(2)}, u32[]{:S(2)}) %collective-permute-start.8) | collective-permute-done | bytes 917536 | tf_op jit(solution)/shard_map/ppermute | solution.py:140
  182.3 4.9 constant_dynamic-slice_fusion
  187.4 3.5 collective-permute-start.11
  194.9 17.6 %collective-permute-done.9 = f32[1,4,112,512]{3,2,1,0:T(8,128)S(1)} collective-permute-done((f32[1,4,112,512]{3,2,1,0:T(8,128)S(1)}, f32[1,4,112,512]{3,2,1,0:T(8,128)S(1)}, u32[]{:S(2)}, u32[]{:S(2)}) %collective-permute-start.9) | collective-permute-done | bytes 917536 | tf_op jit(solution)/shard_map/ppermute | solution.py:140
  217.4 50.4 %collective-permute-done.10 = f32[1,4,112,512]{3,2,1,0:T(8,128)} collective-permute-done((f32[1,4,112,512]{3,2,1,0:T(8,128)}, f32[1,4,112,512]{3,2,1,0:T(8,128)}, u32[]{:S(2)}, u32[]{:S(2)}) %collective-permute-start.10) | collective-permute-done | bytes 917536 | tf_op jit(solution)/shard_map/ppermute | solution.py:140
  270.0 17.4 %collective-permute-done.11 = f32[1,4,112,512]{3,2,1,0:T(8,128)} collective-permute-done((f32[1,4,112,512]{3,2,1,0:T(8,128)}, f32[1,4,112,512]{3,2,1,0:T(8,128)}, u32[]{:S(2)}, u32[]{:S(2)}) %collective-permute-start.11) | collective-permute-done | bytes 917536 | tf_op jit(solution)/shard_map/ppermute | solution.py:140
  293.9 9.4 %collective-permute-done.14 = f32[1,4,112,512]{3,2,1,0:T(8,128)} collective-permute-done((f32[1,4,112,512]{3,2,1,0:T(8,128)S(1)}, f32[1,4,112,512]{3,2,1,0:T(8,128)}, u32[]{:S(2)}, u32[]{:S(2)}) %collective-permute-start.14) | collective-permute-done | bytes 917536 | tf_op jit(solution)/shard_map/ppermute | solution.py:140
  305.4 4.3 copy.413
  309.8 3.8 fusion.289
  313.6 76.2 %conditional.2 = (f32[4,56,4096]{1,0,2:T(4,128)}) conditional(s32[]{:T(128)} %convert_element_type.123, f32[4,56,4096]{2,1,0:T(8,128)} %get-tuple-element.92, (s32[56]{0:T(128)S(1)}, f32[4,56,4096]{2,1,0:T(8,128)}, f32[16,2048]{1,0:T(8,128)S(1)}) %tuple.68), branch_computations={%region_1.2_spmd, %region_2.3_spmd} | conditional | flops 12735988736 | bytes 230196096 | solution.py:127
  316.6 3.5 fusion
  320.1 3.5 fusion.2
  323.6 5.3 fusion.4
  333.9 7.7 %subtract_multiply_fusion = f32[4,56,32,128]{3,2,1,0:T(8,128)S(1)} fusion(f32[4,56,32,128]{3,2,1,0:T(8,128)} %fusion.4, f32[56,32,128]{2,1,0:T(8,128)S(1)} %copy.368, f32[32,4,56,128]{3,0,2,1:T(8,128)} %copy-done.2, f32[32,4,56,128]{3,0,2,1:T(8,128)} %copy-done, f32[32,128]{1,0:T(8,128)S(1)} %get-tuple-element.88, f32[32,128]{1,0:T(8,128)S(1)} %get-tuple-element.89), kind=kOutput, calls=%fused_computation.23 | convolution fusion | flops 1415020544 | bytes 15630336 | tf_op jit(solution)/shard_map/cond/branch_1_fun/brkq,qm->brkm/dot_general | solution.py:88
  351.8 3.5 convolution_add_fusion
  365.4 5.2 multiply_bitcast_fusion
  370.7 4.8 reshape.392
  375.5 5.6 broadcast_select_fusion
  381.1 8.3 %copy.406 = f32[4,56,4096]{1,0,2:T(4,128)} copy(f32[4,56,4096]{2,1,0:T(8,128)} %broadcast_select_fusion) | data formatting | bytes 7340032 | tf_op jit(solution)/shard_map/cond | solution.py:127
  389.8 75.8 %conditional.3 = (f32[4,56,4096]{1,0,2:T(4,128)}) conditional(s32[]{:T(128)} %convert_element_type.125, f32[4,56,4096]{2,1,0:T(8,128)} %get-tuple-element.93, (s32[56]{0:T(128)S(1)}, f32[4,56,4096]{2,1,0:T(8,128)}, f32[16,2048]{1,0:T(8,128)S(1)}) %tuple.69), branch_computations={%region_4.5_spmd, %region_5.6_spmd} | conditional | flops 12735988736 | bytes 230196096 | solution.py:127
  392.6 3.5 fusion.130
  396.1 3.5 fusion.132
  399.6 5.2 fusion.134
  409.5 7.7 %subtract_multiply_fusion.1 = f32[4,56,32,128]{3,2,1,0:T(8,128)S(1)} fusion(f32[4,56,32,128]{3,2,1,0:T(8,128)} %fusion.134, f32[56,32,128]{2,1,0:T(8,128)S(1)} %copy.372, f32[32,4,56,128]{3,0,2,1:T(8,128)} %copy-done.6, f32[32,4,56,128]{3,0,2,1:T(8,128)} %copy-done.4, f32[32,128]{1,0:T(8,128)S(1)} %get-tuple-element.90, f32[32,128]{1,0:T(8,128)S(1)} %get-tuple-element.91), kind=kOutput, calls=%fused_computation.155 | convolution fusion | flops 1415020544 | bytes 15630336 | tf_op jit(solution)/shard_map/cond/branch_1_fun/brkq,qm->brkm/dot_general | solution.py:88
  427.4 3.5 convolution_add_fusion.1
  430.9 3.4 fusion.170
  437.7 3.8 fusion.142
  441.5 5.3 multiply_bitcast_fusion.1
  446.8 4.8 reshape.395
  451.6 5.6 broadcast_select_fusion.1
  457.2 8.2 %copy.408 = f32[4,56,4096]{1,0,2:T(4,128)} copy(f32[4,56,4096]{2,1,0:T(8,128)} %broadcast_select_fusion.1) | data formatting | bytes 7340032 | tf_op jit(solution)/shard_map/cond | solution.py:127
  465.6 8.2 %pad_maximum_fusion = f32[4,112,4096]{1,0,2:T(4,128)S(1)} fusion(f32[4,56,4096]{1,0,2:T(4,128)} %get-tuple-element.80, f32[4,56,4096]{1,0,2:T(4,128)} %get-tuple-element.79), kind=kLoop, calls=%fused_computation.266 | loop fusion | flops 1835008 | bytes 14680064 | tf_op jit(solution)/shard_map/concatenate | solution.py:147
  473.8 143.5 %all_to_all.15 = f32[4,112,4096]{1,0,2:T(4,128)} all-to-all(f32[4,112,4096]{1,0,2:T(4,128)S(1)} %pad_maximum_fusion), channel_id=1, replica_groups=mesh['lat'=4,'lon'=8] {'lon'}, dimensions={2} | all-to-all | bytes 14680064 | tf_op jit(solution)/shard_map/all_to_all | solution.py:148
  617.4 9.5 %copy.388 = f32[8,4,112,512]{3,2,1,0:T(8,128)} copy(f32[8,4,112,512]{2,1,3,0:T(4,128)} %bitcast.200) | data formatting | bytes 14680064 | tf_op jit(solution)/shard_map/all_to_all | solution.py:148
  626.9 10.6 %bitcast_add_fusion = f32[4,8,112,512]{3,2,1,0:T(8,128)} fusion(f32[4,8,112,512]{3,2,1,0:T(8,128)} %param.18, f32[4,8,112,512]{3,2,1,0:T(8,128)} %bitcast.206), kind=kLoop, calls=%fused_computation.268 | loop fusion | flops 1835008 | bytes 22020096 | tf_op jit(solution)/shard_map/add | solution.py:184
  (141 shorter events, 99.7 us)
Async XLA Ops:
  2.6 5.7 copy-start.9
  2.6 61.1 %collective-permute-start.4 = (f32[2,8,1,512]{3,2,1,0:T(1,128)S(1)}, f32[2,8,1,512]{3,2,1,0:T(1,128)S(1)}, u32[]{:S(2)}, u32[]{:S(2)}) collective-permute-start(f32[2,8,1,512]{3,2,1,0:T(1,128)S(1)} %get-tuple-element.107), channel_id=1, source_target_pairs={{8,0},{16,8},{24,16},{9,1},{17,9},{25,17},{10,2},{18,10},{26,18},{... | collective-permute-start | bytes 98312 | tf_op jit(solution)/shard_map/ppermute | solution.py:32
  3.9 12.1 %copy-start.18 = (s32[512]{0:T(512)S(1)}, s32[512]{0:T(512)}, u32[]{:S(2)}) copy-start(s32[512]{0:T(512)} %param.23) | copy-start | bytes 6148
  4.0 59.7 %collective-permute-start.5 = (f32[2,8,1,512]{3,2,1,0:T(1,128)S(1)}, f32[2,8,1,512]{3,2,1,0:T(1,128)S(1)}, u32[]{:S(2)}, u32[]{:S(2)}) collective-permute-start(f32[2,8,1,512]{3,2,1,0:T(1,128)S(1)} %get-tuple-element.108), channel_id=1, source_target_pairs={{0,8},{8,16},{16,24},{1,9},{9,17},{17,25},{2,10},{10,18},{18,26},{... | collective-permute-start | bytes 98312 | tf_op jit(solution)/shard_map/ppermute | solution.py:30
  9.7 52.3 %collective-permute-start = (f32[2,8,112,1]{2,1,3,0:T(8,128)S(1)}, f32[2,8,112,1]{2,1,3,0:T(8,128)S(1)}, u32[]{:S(2)}, u32[]{:S(2)}) collective-permute-start(f32[2,8,112,1]{2,1,3,0:T(8,128)S(1)} %copy.409), channel_id=1, source_target_pairs={{1,0},{2,1},{3,2},{4,3},{5,4},{6,5},{7,6},{0,7},{9,8},{10,9},{11,1... | collective-permute-start | bytes 21512 | tf_op jit(solution)/shard_map/ppermute | solution.py:32
  16.0 46.4 %collective-permute-start.1 = (f32[2,8,112,1]{2,1,3,0:T(8,128)S(1)}, f32[2,8,112,1]{2,1,3,0:T(8,128)S(1)}, u32[]{:S(2)}, u32[]{:S(2)}) collective-permute-start(f32[2,8,112,1]{2,1,3,0:T(8,128)S(1)} %copy.410), channel_id=1, source_target_pairs={{0,1},{1,2},{2,3},{3,4},{4,5},{5,6},{6,7},{7,0},{8,9},{9,10},{10,1... | collective-permute-start | bytes 21512 | tf_op jit(solution)/shard_map/ppermute | solution.py:30
  47.5 14.3 %copy-start.19 = (f32[8]{0:T(128)S(1)}, f32[8]{0:T(128)}, u32[]{:S(2)}) copy-start(f32[8]{0:T(128)} %param.19) | copy-start | bytes 100
  79.1 1.2 copy-start.12
  80.4 56.3 %collective-permute-start.6 = (f32[1,8,1,512]{3,2,1,0:T(1,128)S(1)}, f32[1,8,1,512]{3,2,1,0:T(1,128)S(1)}, u32[]{:S(2)}, u32[]{:S(2)}) collective-permute-start(f32[1,8,1,512]{3,2,1,0:T(1,128)S(1)} %get-tuple-element.112), channel_id=1, source_target_pairs={{8,0},{16,8},{24,16},{9,1},{17,9},{25,17},{10,2},{18,10},{26,18},{... | collective-permute-start | bytes 49160 | tf_op jit(solution)/shard_map/ppermute | solution.py:32
  81.7 55.0 %collective-permute-start.7 = (f32[1,8,1,512]{3,2,1,0:T(1,128)S(1)}, f32[1,8,1,512]{3,2,1,0:T(1,128)S(1)}, u32[]{:S(2)}, u32[]{:S(2)}) collective-permute-start(f32[1,8,1,512]{3,2,1,0:T(1,128)S(1)} %get-tuple-element.111), channel_id=1, source_target_pairs={{0,8},{8,16},{16,24},{1,9},{9,17},{17,25},{2,10},{10,18},{18,26},{... | collective-permute-start | bytes 49160 | tf_op jit(solution)/shard_map/ppermute | solution.py:30
  123.6 13.1 %copy-start.13 = (f32[1,8,112,512]{3,2,1,0:T(8,128)S(1)}, f32[1,8,112,512]{3,2,1,0:T(8,128)}, u32[]{:S(2)}) copy-start(f32[1,8,112,512]{3,2,1,0:T(8,128)} %copy-done.12) | copy-start | bytes 5505028
  131.9 6.7 %copy-start.11 = (f32[1,8,112,512]{3,2,1,0:T(8,128)}, f32[1,8,112,512]{3,2,1,0:T(8,128)S(1)}, u32[]{:S(2)}) copy-start(f32[1,8,112,512]{3,2,1,0:T(8,128)S(1)} %get-tuple-element.86) | copy-start | bytes 5505028
  132.1 18.4 %collective-permute-start.2 = (f32[1,8,112,1]{3,2,1,0:T(8,128)S(1)}, f32[1,8,112,1]{3,2,1,0:T(8,128)S(1)}, u32[]{:S(2)}, u32[]{:S(2)}) collective-permute-start(f32[1,8,112,1]{3,2,1,0:T(8,128)S(1)} %get-tuple-element.113), channel_id=1, source_target_pairs={{1,0},{2,1},{3,2},{4,3},{5,4},{6,5},{7,6},{0,7},{9,8},{10,9},{11,1... | collective-permute-start | bytes 10760 | tf_op jit(solution)/shard_map/ppermute | solution.py:32
  136.7 13.8 %collective-permute-start.3 = (f32[1,8,112,1]{3,2,1,0:T(8,128)S(1)}, f32[1,8,112,1]{3,2,1,0:T(8,128)}, u32[]{:S(2)}, u32[]{:S(2)}) collective-permute-start(f32[1,8,112,1]{3,2,1,0:T(8,128)S(1)} %get-tuple-element.114), channel_id=1, source_target_pairs={{0,1},{1,2},{2,3},{3,4},{4,5},{5,6},{6,7},{7,0},{8,9},{9,10},{10,1... | collective-permute-start | bytes 10760 | tf_op jit(solution)/shard_map/ppermute | solution.py:30
  150.5 4.2 copy-start.10
  150.5 4.2 copy-start.14
  150.5 4.4 copy-start.15
  155.9 3.1 copy-start.8
  159.0 23.3 %collective-permute-start.8 = (f32[1,4,112,512]{3,2,1,0:T(8,128)S(1)}, f32[1,4,112,512]{3,2,1,0:T(8,128)}, u32[]{:S(2)}, u32[]{:S(2)}) collective-permute-start(f32[1,4,112,512]{3,2,1,0:T(8,128)S(1)} %constant_dynamic-slice_fusion.6), channel_id=1, source_target_pairs={{0,1},{1,2},{2,3},{3,4},{4,5},{5,6},{6,7},{7,0},{8,9},{9,10},{10,1... | collective-permute-start | bytes 2752520 | tf_op jit(solution)/shard_map/ppermute | solution.py:140
  160.9 34.0 %copy-start.20 = (s32[112]{0:T(128)S(1)}, s32[112]{0:T(128)}, u32[]{:S(2)}) copy-start(s32[112]{0:T(128)} %param.21) | copy-start | bytes 1348
  160.9 34.0 %copy-start.21 = (s32[112]{0:T(128)S(1)}, s32[112]{0:T(128)}, u32[]{:S(2)}) copy-start(s32[112]{0:T(128)} %param.22) | copy-start | bytes 1348
  187.2 25.2 %collective-permute-start.9 = (f32[1,4,112,512]{3,2,1,0:T(8,128)S(1)}, f32[1,4,112,512]{3,2,1,0:T(8,128)S(1)}, u32[]{:S(2)}, u32[]{:S(2)}) collective-permute-start(f32[1,4,112,512]{3,2,1,0:T(8,128)S(1)} %get-tuple-element.99), channel_id=1, source_target_pairs={{0,2},{1,3},{2,4},{3,5},{4,6},{5,7},{6,0},{7,1},{8,10},{9,11},{10,... | collective-permute-start | bytes 2752520 | tf_op jit(solution)/shard_map/ppermute | solution.py:140
  187.2 80.6 %collective-permute-start.10 = (f32[1,4,112,512]{3,2,1,0:T(8,128)}, f32[1,4,112,512]{3,2,1,0:T(8,128)}, u32[]{:S(2)}, u32[]{:S(2)}) collective-permute-start(f32[1,4,112,512]{3,2,1,0:T(8,128)} %get-tuple-element.98), channel_id=1, source_target_pairs={{0,3},{1,4},{2,5},{3,6},{4,7},{5,0},{6,1},{7,2},{8,11},{9,12},{10,... | collective-permute-start | bytes 2752520 | tf_op jit(solution)/shard_map/ppermute | solution.py:140
  187.4 99.9 %collective-permute-start.11 = (f32[1,4,112,512]{3,2,1,0:T(8,128)}, f32[1,4,112,512]{3,2,1,0:T(8,128)}, u32[]{:S(2)}, u32[]{:S(2)}) collective-permute-start(f32[1,4,112,512]{3,2,1,0:T(8,128)} %get-tuple-element.97), channel_id=1, source_target_pairs={{0,4},{1,5},{2,6},{3,7},{4,0},{5,1},{6,2},{7,3},{8,12},{9,13},{10,... | collective-permute-start | bytes 2752520 | tf_op jit(solution)/shard_map/ppermute | solution.py:140
  190.9 98.6 %collective-permute-start.12 = (f32[1,4,112,512]{3,2,1,0:T(8,128)S(1)}, f32[1,4,112,512]{3,2,1,0:T(8,128)}, u32[]{:S(2)}, u32[]{:S(2)}) collective-permute-start(f32[1,4,112,512]{3,2,1,0:T(8,128)S(1)} %get-tuple-element.96), channel_id=1, source_target_pairs={{0,5},{1,6},{2,7},{3,0},{4,1},{5,2},{6,3},{7,4},{8,13},{9,14},{10,... | collective-permute-start | bytes 2752520 | tf_op jit(solution)/shard_map/ppermute | solution.py:140
  193.3 98.4 %collective-permute-start.13 = (f32[1,4,112,512]{3,2,1,0:T(8,128)S(1)}, f32[1,4,112,512]{3,2,1,0:T(8,128)}, u32[]{:S(2)}, u32[]{:S(2)}) collective-permute-start(f32[1,4,112,512]{3,2,1,0:T(8,128)S(1)} %get-tuple-element.95), channel_id=1, source_target_pairs={{0,6},{1,7},{2,0},{3,1},{4,2},{5,3},{6,4},{7,5},{8,14},{9,15},{10,... | collective-permute-start | bytes 2752520 | tf_op jit(solution)/shard_map/ppermute | solution.py:140
  212.4 0.9 copy-start.16
  212.4 90.8 %collective-permute-start.14 = (f32[1,4,112,512]{3,2,1,0:T(8,128)S(1)}, f32[1,4,112,512]{3,2,1,0:T(8,128)}, u32[]{:S(2)}, u32[]{:S(2)}) collective-permute-start(f32[1,4,112,512]{3,2,1,0:T(8,128)S(1)} %get-tuple-element.94), channel_id=1, source_target_pairs={{0,7},{1,0},{2,1},{3,2},{4,3},{5,4},{6,5},{7,6},{8,15},{9,8},{10,9... | collective-permute-start | bytes 2752520 | tf_op jit(solution)/shard_map/ppermute | solution.py:140
  309.8 3.9 copy-start.17
  320.1 3.5 copy-start
  323.6 5.3 copy-start.2
  341.6 3.3 copy-start.1
  341.7 3.3 copy-start.3
  396.1 3.5 copy-start.4
  399.6 5.2 copy-start.6
  417.2 3.3 copy-start.5
  417.3 3.3 copy-start.7
